TPU v7x, 256 devices: a whole 4x4x8 slice. The times are simulated.
256 devices in a mesh: seq: 32 (over x, z), tp: 8 (over y, core).
Axes of the slice: x: 4, y: 4, z: 8, core: 2. Of those that a mesh axis runs over, the one named last changes fastest.
Arguments:
- tokens: bfloat16 [16384, 5376], P('seq'), may hold values from -6 to 6
- query_weight: bfloat16 [5376, 2048], P(None, 'tp')
- key_weight: bfloat16 [5376, 1024], P(None, 'tp')
- value_weight: bfloat16 [5376, 1024], P(None, 'tp'), may hold values from -0.078125 to 0.078125
- query_norm_gain: float32 [128], replicated, as said below
- key_norm_gain: float32 [128], replicated, as said below
- adapter_down_weight: bfloat16 [32, 5376, 64], P('seq', 'tp'), may hold values from -0.078125 to 0.078125
- adapter_up_weight: bfloat16 [32, 64, 2048], P('seq', None, 'tp'), may hold values from -0.75 to 0.75
- token_adapter_index: int32 [16384, 1], P('seq'), may hold values from 0 to 31; in each aligned block of 512 rows (0 to 511, 512 to 1023, ...) at most 32 rows name the same one
- packed_prompt_length: int32 [16], replicated, may hold values from 1 to 2048, 16384 in all
Outputs:
- attended: bfloat16 [16384, 2048], P('seq', 'tp')
Inputs may be any that keep to these rules, and one draw needn't show every extreme that they name: `token_adapter_index`: in each aligned block of 512 rows (the rows of one index of seq) no adapter is named by more than 32 rows, a bound that some block reaches. `packed_prompt_length`: they sum to 16384; the largest is exactly 2048. `query_norm_gain`: positive gains. `key_norm_gain`: positive gains.
All inputs are finite; a program needn't handle non-finite values.
Results may differ from a plain program's by a relative error of at most 0.02.
Values may be sent and summed in bfloat16 or wider, within the bound.
No kernel may reach another device: no remote copies, remote signals or barrier semaphores. Data moves between devices by JAX's collectives and lax.ppermute only.
A program may use at most 64 MiB of HBM per device.

v0:
```python
import jax
import jax.numpy as jnp
from jax import lax
from jax.sharding import PartitionSpec as P

WINDOW = 1024
query_scale = 0.07715167498104596


def passed_along(block, axis, distance):
    devices = range(lax.axis_size(axis))
    route = [(i - distance, i) for i in devices if i - distance in devices]
    return lax.ppermute(block, axis, route)


def make_dispatch(adapter_of, adapter_total, capacity):
    one_hot = (adapter_of[:, None] == jnp.arange(adapter_total, dtype=jnp.int32)[None, :]).astype(
        jnp.int32
    )
    before = jnp.cumsum(one_hot, axis=0) - one_hot
    slot_index = jnp.sum(before * one_hot, axis=1)
    target = adapter_of * capacity + slot_index
    return (
        jnp.arange(adapter_total * capacity, dtype=jnp.int32)[:, None] == target[None, :]
    ).astype(jnp.bfloat16)


def normalize(field, gain):
    return field / jnp.sqrt(jnp.mean(field * field, axis=-1, keepdims=True) + 1e-06) * gain


def rotate(field, positions):
    half = field.shape[-1] // 2
    freq = jnp.exp(
        -(2.0 * jnp.arange(half, dtype=jnp.float32) / field.shape[-1])
        * jnp.log(jnp.float32(10000.0))
    )
    angle = positions[:, None] * freq[None, :]
    cosine = jnp.cos(angle)[:, None, :]
    sine = jnp.sin(angle)[:, None, :]
    first = field[..., :half]
    second = field[..., half:]
    return jnp.concatenate(
        [first * cosine - second * sine, second * cosine + first * sine], axis=-1
    )


def body(
    tokens,
    query_weight,
    key_weight,
    value_weight,
    query_norm_gain,
    key_norm_gain,
    adapter_down_weight,
    adapter_up_weight,
    token_adapter_index,
    packed_prompt_length,
):
    rows = tokens.shape[0]
    head_dim = query_norm_gain.shape[0]
    kv_local = key_weight.shape[1] // head_dim
    q_local = query_weight.shape[1] // head_dim
    groups = q_local // kv_local
    seq_count = lax.axis_size("seq")
    owned_rows = adapter_down_weight.shape[0]
    adapter_total = owned_rows * seq_count
    capacity = 2 * rows // adapter_total
    feature_slice = adapter_down_weight.shape[1]
    seq_index = lax.axis_index("seq")
    tp_index = lax.axis_index("tp")
    dispatch = make_dispatch(token_adapter_index[:, 0], adapter_total, capacity)
    x_part = lax.dynamic_slice_in_dim(tokens, tp_index * feature_slice, feature_slice, 1)
    packed = jnp.dot(dispatch, x_part, preferred_element_type=jnp.float32).astype(jnp.bfloat16)
    down_all, up_all = (
        lax.all_gather(adapter_down_weight, "seq", axis=0, tiled=True),
        lax.all_gather(adapter_up_weight, "seq", axis=0, tiled=True),
    )
    packed = packed.reshape(adapter_total, capacity, feature_slice)
    partial_low = jnp.einsum("acd,adr->acr", packed, down_all, preferred_element_type=jnp.float32)
    low_rank = lax.psum(partial_low, "tp").astype(jnp.bfloat16)
    delta_slots = jnp.einsum(
        "acr,are->ace", low_rank, up_all, preferred_element_type=jnp.float32
    ).astype(jnp.bfloat16)
    delta_slots = delta_slots.reshape(adapter_total * capacity, q_local * head_dim)
    delta_rows = jnp.einsum("st,se->te", dispatch, delta_slots, preferred_element_type=jnp.float32)
    query = jnp.dot(tokens, query_weight, preferred_element_type=jnp.float32) + delta_rows
    keys = jnp.dot(tokens, key_weight, preferred_element_type=jnp.float32)
    values = jnp.dot(tokens, value_weight, preferred_element_type=jnp.float32).astype(jnp.bfloat16)
    positions = seq_index * rows + jnp.arange(rows, dtype=jnp.int32)
    pos_float = positions.astype(jnp.float32)
    query_rot = rotate(
        normalize(query.reshape(rows, q_local, head_dim), query_norm_gain), pos_float
    ).astype(jnp.bfloat16)
    key_rot = rotate(
        normalize(keys.reshape(rows, kv_local, head_dim), key_norm_gain), pos_float
    ).astype(jnp.bfloat16)
    reach = WINDOW // rows
    earlier = []
    for offset in range(reach, 0, -1):
        earlier.append(passed_along((key_rot, values), "seq", offset))
    all_keys = jnp.concatenate([piece[0] for piece in earlier] + [key_rot], axis=0)
    all_values = jnp.concatenate([piece[1] for piece in earlier] + [values], axis=0)
    all_values = all_values.reshape(WINDOW + rows, kv_local, head_dim)
    key_pos = seq_index * rows - WINDOW + jnp.arange(WINDOW + rows, dtype=jnp.int32)
    starts = jnp.cumsum(packed_prompt_length) - packed_prompt_length
    prompt_start = jnp.max(
        jnp.where(starts[None, :] <= positions[:, None], starts[None, :], 0), axis=1
    )
    lower = jnp.maximum(positions - WINDOW + 1, prompt_start)
    allowed = (key_pos[None, :] >= lower[:, None]) & (key_pos[None, :] <= positions[:, None])
    query_four = query_rot.reshape(rows, kv_local, groups, head_dim)
    scores = (
        jnp.einsum("tkgd,skd->kgts", query_four, all_keys, preferred_element_type=jnp.float32)
        * query_scale
    )
    scores = jnp.where(allowed[None, None], scores, jnp.float32(-1e30))
    peak = jnp.max(scores, axis=-1, keepdims=True)
    weights = jnp.exp(scores - peak)
    probs = (weights / jnp.sum(weights, axis=-1, keepdims=True)).astype(jnp.bfloat16)
    mixed = jnp.einsum("kgts,skd->tkgd", probs, all_values, preferred_element_type=jnp.float32)
    return mixed.astype(jnp.bfloat16).reshape(rows, q_local * head_dim)


def solution(mesh):
    in_specs = (
        P("seq", None),
        P(None, "tp"),
        P(None, "tp"),
        P(None, "tp"),
        P(),
        P(),
        P("seq", "tp", None),
        P("seq", None, "tp"),
        P("seq", None),
        P(),
    )
    out_specs = P("seq", "tp")
    return jax.shard_map(body, mesh=mesh, in_specs=in_specs, out_specs=out_specs, check_vma=False)
```

profile of v0, /device:TPU:8, one launch (start us, length us, event | category | flops | bytes accessed | tf_op | source)
XLA Modules:
  0.0 193.4 jit_solution(9777939212335164480)
XLA Ops:
  6.5 0.7 all-gather.3.cloned.1.call-update
  7.4 5.1 %multiply_reduce_fusion.1 = (f32[512]{0:T(512)S(1)}, f32[512,128]{0,1:T(8,128)S(1)}) fusion(bf16[512,5376]{1,0:T(8,128)(2,1)} %param.10, bf16[5376,128]{1,0:T(8,128)(2,1)} %param.12), kind=kOutput, calls=%fused_computation.43 | convolution fusion | flops 704773632 | bytes 7145472 | tf_op jit(solution)/shard_map/dot_general | solution.py:88
  12.6 0.6 fusion.34
  13.2 0.6 copy-done.2
  13.8 0.7 pad_maximum_fusion
  14.4 5.8 %collective-permute-start.2 = (bf16[512,1,128]{0,2,1:T(8,128)(2,1)}, bf16[512,1,128]{0,2,1:T(8,128)(2,1)}, u32[]{:S(2)}, u32[]{:S(2)}) collective-permute-start(bf16[512,1,128]{0,2,1:T(8,128)(2,1)} %pad_maximum_fusion), channel_id=1, source_target_pairs={{0,16},{8,24},{16,32},{24,40},{32,48},{40,56},{48,64},{56,72},{64,... | collective-permute-start | bytes 393224 | tf_op jit(solution)/shard_map/ppermute | solution.py:13
  20.2 4.5 %collective-permute-start.3 = (bf16[512,1,128]{0,2,1:T(8,128)(2,1)}, bf16[512,1,128]{0,2,1:T(8,128)(2,1)}, u32[]{:S(2)}, u32[]{:S(2)}) collective-permute-start(bf16[512,1,128]{0,2,1:T(8,128)(2,1)} %pad_maximum_fusion), channel_id=1, source_target_pairs={{0,8},{8,16},{16,24},{24,32},{32,40},{40,48},{48,56},{56,64},{64,7... | collective-permute-start | bytes 393224 | tf_op jit(solution)/shard_map/ppermute | solution.py:13
  24.7 2.2 %convolution_convert_fusion.1 = bf16[512,128]{1,0:T(8,128)(2,1)} fusion(bf16[512,5376]{1,0:T(8,128)(2,1)S(1)} %copy-done.1, bf16[5376,128]{1,0:T(8,128)(2,1)S(1)} %copy-done.8), kind=kOutput, calls=%fused_computation.15 | convolution fusion | flops 704708608 | bytes 7012352 | tf_op jit(solution)/shard_map/dot_general | solution.py:89
  27.0 4.9 %collective-permute-start = (bf16[512,128]{1,0:T(8,128)(2,1)}, bf16[512,128]{1,0:T(8,128)(2,1)}, u32[]{:S(2)}, u32[]{:S(2)}) collective-permute-start(bf16[512,128]{1,0:T(8,128)(2,1)} %convolution_convert_fusion.1), channel_id=1, source_target_pairs={{0,16},{8,24},{16,32},{24,40},{32,48},{40,56},{48,64},{56,72},{64,... | collective-permute-start | bytes 393224 | tf_op jit(solution)/shard_map/ppermute | solution.py:13
  31.8 3.6 %collective-permute-start.1 = (bf16[512,128]{1,0:T(8,128)(2,1)}, bf16[512,128]{1,0:T(8,128)(2,1)}, u32[]{:S(2)}, u32[]{:S(2)}) collective-permute-start(bf16[512,128]{1,0:T(8,128)(2,1)} %convolution_convert_fusion.1), channel_id=1, source_target_pairs={{0,8},{8,16},{16,24},{24,32},{32,40},{40,48},{48,56},{56,64},{64,7... | collective-permute-start | bytes 393224 | tf_op jit(solution)/shard_map/ppermute | solution.py:13
  35.5 1.2 reduce-window.20
  36.6 0.2 slice_reduce_fusion
  36.9 0.1 fusion.39
  37.1 0.1 reduce.4
  37.3 3.5 %fusion.6 = bf16[1024,672]{0,1:T(8,128)(2,1)} fusion(s32[512]{0:T(512)S(1)} %multiply_add_fusion, bf16[512,5376]{1,0:T(8,128)(2,1)} %param.10, s32[]{:T(128)S(6)} %select_n.12), kind=kOutput, calls=%fused_computation.11 | convolution fusion | flops 705855488 | bytes 2164740 | tf_op jit(solution)/shard_map/dot_general | solution.py:74
  40.9 2.5 %copy.35 = bf16[1024,672]{1,0:T(8,128)(2,1)} copy(bf16[1024,672]{0,1:T(8,128)(2,1)} %fusion.6) | data formatting | bytes 2752512 | tf_op jit(solution)/shard_map/convert_element_type | solution.py:74
  43.5 1.8 multiply_cosine_fusion
  45.3 0.7 compare_and_fusion
  46.0 5.0 %fusion.47 = f32[512,256]{0,1:T(8,128)} fusion(bf16[512,5376]{1,0:T(8,128)(2,1)} %param.10, bf16[5376,256]{1,0:T(8,128)(2,1)S(1)} %copy-done), kind=kOutput, calls=%fused_computation.78 | convolution fusion | flops 1409286144 | bytes 8781824 | tf_op jit(solution)/shard_map/dot_general | solution.py:87
  51.0 41.4 %all-gather.3.cloned.1.call-done = bf16[32,672,64]{1,2,0:T(8,128)(2,1)} async-done(((bf16[1,672,64]{1,2,0:T(8,128)(2,1)}), bf16[32,672,64]{1,2,0:T(8,128)(2,1)}) %all-gather.3.cloned.1.call-update) | async-done | bytes 2752528 | tf_op jit(solution)/shard_map/all_gather | solution.py:76
  92.4 4.1 %fusion.48 = f32[32,32,64]{2,1,0:T(8,128)} fusion(bf16[32,32,672]{2,1,0:T(8,128)(2,1)} %bitcast.74, bf16[32,672,64]{1,2,0:T(8,128)(2,1)} %all-gather.3.cloned.1.call-done), kind=kOutput, calls=%fused_computation.79 | convolution fusion | flops 88080384 | bytes 4390912 | tf_op jit(solution)/shard_map/acd,adr->acr/dot_general | solution.py:80
  96.5 27.3 %all-reduce.1 = bf16[32,32,64]{2,1,0:T(8,128)(2,1)} all-reduce(f32[32,32,64]{2,1,0:T(8,128)} %fusion.48), channel_id=1, replica_groups=mesh['seq'=32,'tp'=8] {'tp'}, use_global_device_ids=true, to_apply=%region_6.7 | all-reduce | flops 65536 | bytes 393216 | tf_op jit(solution)/shard_map/psum | solution.py:81
  123.8 44.2 %all-gather.5.cloned.1.call-done = bf16[32,64,256]{2,1,0:T(8,128)(2,1)} async-done(((bf16[1,64,256]{2,1,0:T(8,128)(2,1)}), bf16[32,64,256]{2,1,0:T(8,128)(2,1)}) %all-gather.5.cloned.1.call-update) | async-done | bytes 1048592 | tf_op jit(solution)/shard_map/all_gather | solution.py:77
  167.9 1.6 convolution_convert_fusion
  169.6 2.5 %multiply_reduce_fusion = (f32[512,2]{0,1:T(2,128)S(1)}, f32[512,256]{0,1:T(8,128)}) fusion(f32[512,256]{0,1:T(8,128)} %fusion.47, bf16[1024,256]{1,0:T(8,128)(2,1)S(1)} %bitcast.75, s32[512]{0:T(512)S(1)} %multiply_add_fusion), kind=kOutput, calls=%fused_computation.22 | convolution fusion | flops 269351936 | bytes 1579008 | tf_op jit(solution)/shard_map/st,se->te/dot_general | solution.py:86
  172.0 2.0 %copy.36 = f32[512,2,128]{2,0,1:T(8,128)} copy(f32[512,2,128]{0,2,1:T(8,128)} %bitcast.76) | data formatting | bytes 1048576 | tf_op jit(solution)/shard_map/reshape | solution.py:93
  174.1 1.2 divide_multiply_fusion
  175.3 1.3 subtract_convert_fusion
  176.6 2.7 %fusion.1 = (f32[2,512]{1,0:T(2,128)S(1)}, f32[1536,512,2]{1,0,2:T(8,128)S(1)}) fusion(pred[512,1536]{0,1:T(8,128)(4,1)S(1)} %compare_and_fusion, bf16[512,2,64]{2,0,1:T(8,128)(2,1)S(1)} %get-tuple-element.6, bf16[512,2,64]{2,0,1:T(8,128)(2,1)S(1)} %get-tuple-element.5, bf16[512,1,64]{0,2,1:T(8,128)(2,1)} %copy-done.3, bf16[512,1,64]{0,2,1:T(8,128)(2,1)} %copy-done.2, ...), kind=kOutput, calls=%fused_computation.4 | convolution fusion | flops 409467904 | bytes 7737344 | tf_op jit(solution)/shard_map/tkgd,skd->kgts/dot_general | solution.py:114
  179.3 1.5 fusion
  180.8 3.9 %fusion.8 = bf16[128,2,512]{2,0,1:T(8,128)(2,1)} fusion(f32[2,512]{1,0:T(2,128)S(1)} %fusion, f32[2,512]{1,0:T(2,128)S(1)} %get-tuple-element.15, f32[1536,512,2]{1,0,2:T(8,128)S(1)} %get-tuple-element.16, pred[512,1536]{0,1:T(8,128)(4,1)S(1)} %compare_and_fusion, bf16[512,128]{1,0:T(8,128)(2,1)} %convolution_convert_fusion.1, ...), kind=kOutput, calls=%fused_computation.14 | convolution fusion | flops 411828224 | bytes 7741440 | tf_op jit(solution)/shard_map/kgts,skd->tkgd/dot_general | solution.py:121
  184.7 1.8 copy.40
  (40 shorter events, 0.5 us)
Async XLA Ops:
  6.5 39.4 %copy-start = (bf16[5376,256]{1,0:T(8,128)(2,1)S(1)}, bf16[5376,256]{1,0:T(8,128)(2,1)}, u32[]{:S(2)}) copy-start(bf16[5376,256]{1,0:T(8,128)(2,1)} %param.11) | copy-start | bytes 8257540
  6.5 5.9 %copy-start.5 = (f32[128]{0:T(128)S(1)}, f32[128]{0:T(128)}, u32[]{:S(2)}) copy-start(f32[128]{0:T(128)} %param.15) | copy-start | bytes 1540
  6.5 85.9 %all-gather.3.cloned.1.call-start = ((), (), s32[]{:S(2)}) async-start(), calls=%async_computation | async-start | bytes 3244032 | tf_op jit(solution)/shard_map/all_gather | solution.py:76
  7.3 160.7 %all-gather.5.cloned.1.call-start = ((), (), s32[]{:S(2)}) async-start(), calls=%async_computation.1 | async-start | bytes 1081344 | tf_op jit(solution)/shard_map/all_gather | solution.py:77
  7.3 17.4 %copy-start.1 = (bf16[512,5376]{1,0:T(8,128)(2,1)S(1)}, bf16[512,5376]{1,0:T(8,128)(2,1)}, u32[]{:S(2)}) copy-start(bf16[512,5376]{1,0:T(8,128)(2,1)} %param.10) | copy-start | bytes 16515076
  7.4 17.4 %copy-start.8 = (bf16[5376,128]{1,0:T(8,128)(2,1)S(1)}, bf16[5376,128]{1,0:T(8,128)(2,1)}, u32[]{:S(2)}) copy-start(bf16[5376,128]{1,0:T(8,128)(2,1)} %param.13) | copy-start | bytes 4128772
  12.4 23.0 %copy-start.4 = (s32[512,1]{0,1:T(1,128)S(1)}, s32[512,1]{0,1:T(1,128)}, u32[]{:S(2)}) copy-start(s32[512,1]{0,1:T(1,128)} %param.18) | copy-start | bytes 6148
  12.4 24.6 %copy-start.7 = (s32[16]{0:T(128)S(1)}, s32[16]{0:T(128)}, u32[]{:S(2)}) copy-start(s32[16]{0:T(128)} %param.19) | copy-start | bytes 196
  13.1 0.6 copy-start.2
  13.2 1.3 copy-start.3
  14.4 162.2 %collective-permute-start.2 = (bf16[512,1,128]{0,2,1:T(8,128)(2,1)}, bf16[512,1,128]{0,2,1:T(8,128)(2,1)}, u32[]{:S(2)}, u32[]{:S(2)}) collective-permute-start(bf16[512,1,128]{0,2,1:T(8,128)(2,1)} %pad_maximum_fusion), channel_id=1, source_target_pairs={{0,16},{8,24},{16,32},{24,40},{32,48},{40,56},{48,64},{56,72},{64,... | collective-permute-start | bytes 393224 | tf_op jit(solution)/shard_map/ppermute | solution.py:13
  20.2 156.4 %collective-permute-start.3 = (bf16[512,1,128]{0,2,1:T(8,128)(2,1)}, bf16[512,1,128]{0,2,1:T(8,128)(2,1)}, u32[]{:S(2)}, u32[]{:S(2)}) collective-permute-start(bf16[512,1,128]{0,2,1:T(8,128)(2,1)} %pad_maximum_fusion), channel_id=1, source_target_pairs={{0,8},{8,16},{16,24},{24,32},{32,40},{40,48},{48,56},{56,64},{64,7... | collective-permute-start | bytes 393224 | tf_op jit(solution)/shard_map/ppermute | solution.py:13
  27.0 153.8 %collective-permute-start = (bf16[512,128]{1,0:T(8,128)(2,1)}, bf16[512,128]{1,0:T(8,128)(2,1)}, u32[]{:S(2)}, u32[]{:S(2)}) collective-permute-start(bf16[512,128]{1,0:T(8,128)(2,1)} %convolution_convert_fusion.1), channel_id=1, source_target_pairs={{0,16},{8,24},{16,32},{24,40},{32,48},{40,56},{48,64},{56,72},{64,... | collective-permute-start | bytes 393224 | tf_op jit(solution)/shard_map/ppermute | solution.py:13
  31.8 149.0 %collective-permute-start.1 = (bf16[512,128]{1,0:T(8,128)(2,1)}, bf16[512,128]{1,0:T(8,128)(2,1)}, u32[]{:S(2)}, u32[]{:S(2)}) collective-permute-start(bf16[512,128]{1,0:T(8,128)(2,1)} %convolution_convert_fusion.1), channel_id=1, source_target_pairs={{0,8},{8,16},{16,24},{24,32},{32,40},{40,48},{48,56},{56,64},{64,7... | collective-permute-start | bytes 393224 | tf_op jit(solution)/shard_map/ppermute | solution.py:13
  51.0 123.1 %copy-start.6 = (f32[128]{0:T(128)S(1)}, f32[128]{0:T(128)}, u32[]{:S(2)}) copy-start(f32[128]{0:T(128)} %param.14) | copy-start | bytes 1540
Sparse Core Ops, SparseCore 0:
  9.9 82.4 all-gather.2
  95.0 72.9 all-gather.4
where the time goes:
time: 194 us; the launch traced here: 193 us
  waiting for transfers between devices  86.3 us (44%)
  matrix products  30.6 us (16%)
  blocking collectives  27.3 us (14%)
  starting transfers between devices  18.8 us (10%)
  between operations  13.6 us (7%)
  other arithmetic  9.43 us (5%)
  local copies, waits for them, and re-layouts  7.32 us (4%)
    all_gather x1, waiting for transfers between devices, body(): lax.all_gather(adapter_up_weight, 'seq', axis=0, tiled=True)  44.2 us
    all_gather x1, waiting for transfers between devices, body(): lax.all_gather(adapter_down_weight, 'seq', axis=0, tiled=True)  41.4 us
    psum x1, blocking collectives, body(): low_rank = lax.psum(partial_low, 'tp').astype(jnp.bfloat16)  27.3 us
    ppermute x4, starting transfers between devices, passed_along(): return lax.ppermute(block, axis, route)  18.7 us
    dot_general x1, matrix products, body(): keys = jnp.dot(tokens, key_weight, preferred_element_type=jnp.float32)  5.07 us
    dot_general x1, matrix products, body(): jnp.dot(tokens, query_weight, preferred_element_type=jnp.float32)  5.02 us
    dot_general x1, matrix products, body(): jnp.einsum('acd,adr->acr', packed, down_all, preferred_element_type=jnp.f...  4.11 us
    dot_general x1, matrix products, body(): jnp.einsum('kgts,skd->tkgd', probs, all_values, preferred_element_type=jn...  3.91 us
  transfers between devices with their start and end apart: 6, of which 2 were waited for; matrix products, arithmetic and copies ran while one was open for 21% of the time, Pallas kernels for 0%

commit v1 on v0

--- a/solution.py
+++ b/solution.py
@@ -1,3 +1,4 @@
+import functools
 import jax
 import jax.numpy as jnp
 from jax import lax
@@ -5,6 +6,13 @@
 
 WINDOW = 1024
 query_scale = 0.07715167498104596
+
+
+def shape_the_pipes(original, axis_key):
+    return lax.all_gather(original, axis_name=axis_key).sum(axis=0)
+
+
+choose_cards = functools.partial(shape_the_pipes, axis_key="tp")
 
 
 def passed_along(block, axis, distance):
@@ -78,7 +86,7 @@
     )
     packed = packed.reshape(adapter_total, capacity, feature_slice)
     partial_low = jnp.einsum("acd,adr->acr", packed, down_all, preferred_element_type=jnp.float32)
-    low_rank = lax.psum(partial_low, "tp").astype(jnp.bfloat16)
+    low_rank = choose_cards(partial_low).astype(jnp.bfloat16)
     delta_slots = jnp.einsum(
         "acr,are->ace", low_rank, up_all, preferred_element_type=jnp.float32
     ).astype(jnp.bfloat16)

time: 194 us -> 232 us (1.20)
  waiting for transfers between devices: 86.3 us -> 148 us
  blocking collectives: 27.3 us -> 0 us
  other arithmetic: 9.43 us -> 15 us
  starting transfers between devices: 18.8 us -> 15 us
  matrix products: 30.6 us -> 33.6 us
    all_gather x1, waiting for transfers between devices: 41.4 us -> 75.2 us  [body(): lax.all_gather(adapter_down_weight, 'seq', axis=0, tiled=True)]
    all_gather x1, waiting for transfers between devices: 44.2 us -> 71.7 us  [body(): lax.all_gather(adapter_up_weight, 'seq', axis=0, tiled=True)]
    psum x1 -> x0, blocking collectives: 27.3 us -> none  [body(): low_rank = lax.psum(partial_low, 'tp').astype(jnp.bfloat16)]
    ppermute x4, starting transfers between devices: 18.7 us -> 14.9 us  [passed_along(): return lax.ppermute(block, axis, route)]
    reduce_sum x0 -> x1, other arithmetic: none -> 3.49 us  [shape_the_pipes(): return lax.all_gather(original, axis_name=axis_key).sum(axis=0)]
    dot_general x1, matrix products: 2.23 us -> 5.37 us  [body(): jnp.dot(tokens, value_weight, preferred_element_type=jnp.float32)]
  transfers between devices with their start and end apart: 6 -> 7, of which waited for: 2 -> 2; matrix products, arithmetic and copies ran while one was open for 21% -> 20% of each run, Pallas kernels for 0% -> 0%
where the time goes in v1:
time: 232 us
  waiting for transfers between devices  148 us (64%)
  matrix products  33.6 us (14%)
  starting transfers between devices  15 us (6%)
  other arithmetic  15 us (6%)
  between operations  13.3 us (6%)
  local copies, waits for them, and re-layouts  7.3 us (3%)
    all_gather x1, waiting for transfers between devices, body(): lax.all_gather(adapter_down_weight, 'seq', axis=0, tiled=True)  75.2 us
    all_gather x1, waiting for transfers between devices, body(): lax.all_gather(adapter_up_weight, 'seq', axis=0, tiled=True)  71.7 us
    ppermute x4, starting transfers between devices, passed_along(): return lax.ppermute(block, axis, route)  14.9 us
    dot_general x1, matrix products, body(): jnp.dot(tokens, value_weight, preferred_element_type=jnp.float32)  5.37 us
    dot_general x1, matrix products, body(): jnp.dot(tokens, query_weight, preferred_element_type=jnp.float32)  5 us
    dot_general x1, matrix products, body(): keys = jnp.dot(tokens, key_weight, preferred_element_type=jnp.float32)  4.92 us
  transfers between devices with their start and end apart: 7, of which 2 were waited for; matrix products, arithmetic and copies ran while one was open for 20% of the time, Pallas kernels for 0%

profile of v1, /device:TPU:8, one launch (start us, length us, event | category | flops | bytes accessed | tf_op | source)
XLA Modules:
  0.0 231.8 jit_solution(1550406330233095189)
XLA Ops:
  6.5 0.7 all-gather.5.cloned.1.call-update
  7.3 0.7 fusion.40
  8.1 1.2 reduce-window.20
  9.5 0.8 fusion.39
  10.3 0.7 multiply_add_fusion
  10.9 3.5 %fusion.6 = bf16[1024,672]{0,1:T(8,128)(2,1)} fusion(s32[512]{0:T(512)S(1)} %multiply_add_fusion, bf16[512,5376]{1,0:T(8,128)(2,1)} %param.10, s32[]{:T(128)S(6)} %select_n.12), kind=kOutput, calls=%fused_computation.11 | convolution fusion | flops 705855488 | bytes 2164740 | tf_op jit(solution)/shard_map/dot_general | solution.py:82
  14.5 2.5 %copy.36 = bf16[1024,672]{1,0:T(8,128)(2,1)} copy(bf16[1024,672]{0,1:T(8,128)(2,1)} %fusion.6) | data formatting | bytes 2752512 | tf_op jit(solution)/shard_map/convert_element_type | solution.py:82
  17.0 75.2 %all-gather.5.cloned.1.call-done = bf16[32,672,64]{1,2,0:T(8,128)(2,1)} async-done(((bf16[1,672,64]{1,2,0:T(8,128)(2,1)}), bf16[32,672,64]{1,2,0:T(8,128)(2,1)}) %all-gather.5.cloned.1.call-update) | async-done | bytes 2752528 | tf_op jit(solution)/shard_map/all_gather | solution.py:84
  92.2 4.1 %fusion.48 = f32[32,32,64]{2,1,0:T(8,128)} fusion(bf16[32,32,672]{2,1,0:T(8,128)(2,1)} %bitcast.75, bf16[32,672,64]{1,2,0:T(8,128)(2,1)} %all-gather.5.cloned.1.call-done), kind=kOutput, calls=%fused_computation.79 | convolution fusion | flops 88080384 | bytes 4390912 | tf_op jit(solution)/shard_map/acd,adr->acr/dot_general | solution.py:88
  96.4 4.9 %multiply_reduce_fusion.1 = (f32[512]{0:T(512)S(1)}, f32[512,128]{0,1:T(8,128)S(1)}) fusion(bf16[512,5376]{1,0:T(8,128)(2,1)} %param.10, bf16[5376,128]{1,0:T(8,128)(2,1)} %param.12), kind=kOutput, calls=%fused_computation.43 | convolution fusion | flops 704773632 | bytes 7145472 | tf_op jit(solution)/shard_map/dot_general | solution.py:96
  101.5 0.6 fusion.34
  102.1 0.6 copy-done.1
  102.7 0.7 pad_maximum_fusion
  103.3 3.9 %collective-permute-start.2 = (bf16[512,1,128]{0,2,1:T(8,128)(2,1)}, bf16[512,1,128]{0,2,1:T(8,128)(2,1)}, u32[]{:S(2)}, u32[]{:S(2)}) collective-permute-start(bf16[512,1,128]{0,2,1:T(8,128)(2,1)} %pad_maximum_fusion), channel_id=1, source_target_pairs={{0,16},{8,24},{16,32},{24,40},{32,48},{40,56},{48,64},{56,72},{64,... | collective-permute-start | bytes 393224 | tf_op jit(solution)/shard_map/ppermute | solution.py:21
  107.2 4.6 %collective-permute-start.3 = (bf16[512,1,128]{0,2,1:T(8,128)(2,1)}, bf16[512,1,128]{0,2,1:T(8,128)(2,1)}, u32[]{:S(2)}, u32[]{:S(2)}) collective-permute-start(bf16[512,1,128]{0,2,1:T(8,128)(2,1)} %pad_maximum_fusion), channel_id=1, source_target_pairs={{0,8},{8,16},{16,24},{24,32},{32,40},{40,48},{48,56},{56,64},{64,7... | collective-permute-start | bytes 393224 | tf_op jit(solution)/shard_map/ppermute | solution.py:21
  111.9 5.4 %convolution_convert_fusion.1 = bf16[512,128]{1,0:T(8,128)(2,1)} fusion(bf16[512,5376]{1,0:T(8,128)(2,1)} %param.10, bf16[5376,128]{1,0:T(8,128)(2,1)} %param.13), kind=kOutput, calls=%fused_computation.15 | convolution fusion | flops 704708608 | bytes 7012352 | tf_op jit(solution)/shard_map/dot_general | solution.py:97
  117.2 2.7 %collective-permute-start = (bf16[512,128]{1,0:T(8,128)(2,1)}, bf16[512,128]{1,0:T(8,128)(2,1)}, u32[]{:S(2)}, u32[]{:S(2)}) collective-permute-start(bf16[512,128]{1,0:T(8,128)(2,1)} %convolution_convert_fusion.1), channel_id=1, source_target_pairs={{0,16},{8,24},{16,32},{24,40},{32,48},{40,56},{48,64},{56,72},{64,... | collective-permute-start | bytes 393224 | tf_op jit(solution)/shard_map/ppermute | solution.py:21
  119.9 3.7 %collective-permute-start.1 = (bf16[512,128]{1,0:T(8,128)(2,1)}, bf16[512,128]{1,0:T(8,128)(2,1)}, u32[]{:S(2)}, u32[]{:S(2)}) collective-permute-start(bf16[512,128]{1,0:T(8,128)(2,1)} %convolution_convert_fusion.1), channel_id=1, source_target_pairs={{0,8},{8,16},{16,24},{24,32},{32,40},{40,48},{48,56},{56,64},{64,7... | collective-permute-start | bytes 393224 | tf_op jit(solution)/shard_map/ppermute | solution.py:21
  124.0 1.8 multiply_cosine_fusion
  125.8 0.7 compare_and_fusion
  126.5 5.0 %fusion.47 = f32[512,256]{0,1:T(8,128)} fusion(bf16[512,5376]{1,0:T(8,128)(2,1)} %param.10, bf16[5376,256]{1,0:T(8,128)(2,1)S(1)} %copy-done), kind=kOutput, calls=%fused_computation.78 | convolution fusion | flops 1409286144 | bytes 8781824 | tf_op jit(solution)/shard_map/dot_general | solution.py:95
  131.5 3.5 %reduce_sum.47 = bf16[32,32,64]{2,1,0:T(8,128)(2,1)} reduce(f32[8,32,32,64]{3,2,1,0:T(8,128)} %bitcast.76, f32[]{:T(128)} %constant.16.clone.1), dimensions={0}, to_apply=%region_6.7 | reduce | flops 458752 | bytes 2228228 | tf_op jit(solution)/shard_map/reduce_sum | solution.py:12
  135.0 71.7 %all-gather.7.cloned.1.call-done = bf16[32,64,256]{2,1,0:T(8,128)(2,1)} async-done(((bf16[1,64,256]{2,1,0:T(8,128)(2,1)}), bf16[32,64,256]{2,1,0:T(8,128)(2,1)}) %all-gather.7.cloned.1.call-update) | async-done | bytes 1048592 | tf_op jit(solution)/shard_map/all_gather | solution.py:85
  206.7 1.6 convolution_convert_fusion
  208.3 2.5 %multiply_reduce_fusion = (f32[512,2]{0,1:T(2,128)S(1)}, f32[512,256]{0,1:T(8,128)}) fusion(f32[512,256]{0,1:T(8,128)} %fusion.47, bf16[1024,256]{1,0:T(8,128)(2,1)S(1)} %bitcast.77, s32[512]{0:T(512)S(1)} %multiply_add_fusion), kind=kOutput, calls=%fused_computation.22 | convolution fusion | flops 269351936 | bytes 1579008 | tf_op jit(solution)/shard_map/st,se->te/dot_general | solution.py:94
  210.7 2.0 copy.37
  212.8 1.2 divide_multiply_fusion
  214.0 1.3 subtract_convert_fusion
  215.3 2.7 %fusion.1 = (f32[2,512]{1,0:T(2,128)S(1)}, f32[1536,512,2]{1,0,2:T(8,128)S(1)}) fusion(pred[512,1536]{0,1:T(8,128)(4,1)S(1)} %compare_and_fusion, bf16[512,2,64]{2,0,1:T(8,128)(2,1)S(1)} %get-tuple-element.6, bf16[512,2,64]{2,0,1:T(8,128)(2,1)S(1)} %get-tuple-element.5, bf16[512,1,64]{0,2,1:T(8,128)(2,1)} %copy-done.2, bf16[512,1,64]{0,2,1:T(8,128)(2,1)} %copy-done.1, ...), kind=kOutput, calls=%fused_computation.4 | convolution fusion | flops 409467904 | bytes 7737344 | tf_op jit(solution)/shard_map/tkgd,skd->kgts/dot_general | solution.py:122
  218.0 1.5 fusion
  219.5 3.9 %fusion.8 = bf16[128,2,512]{2,0,1:T(8,128)(2,1)} fusion(f32[2,512]{1,0:T(2,128)S(1)} %fusion, f32[2,512]{1,0:T(2,128)S(1)} %get-tuple-element.15, f32[1536,512,2]{1,0,2:T(8,128)S(1)} %get-tuple-element.16, pred[512,1536]{0,1:T(8,128)(4,1)S(1)} %compare_and_fusion, bf16[512,128]{1,0:T(8,128)(2,1)} %convolution_convert_fusion.1, ...), kind=kOutput, calls=%fused_computation.14 | convolution fusion | flops 411828224 | bytes 7741440 | tf_op jit(solution)/shard_map/kgts,skd->tkgd/dot_general | solution.py:129
  223.4 1.8 copy.41
  (37 shorter events, 0.9 us)
Async XLA Ops:
  6.5 119.9 %copy-start = (bf16[5376,256]{1,0:T(8,128)(2,1)S(1)}, bf16[5376,256]{1,0:T(8,128)(2,1)}, u32[]{:S(2)}) copy-start(bf16[5376,256]{1,0:T(8,128)(2,1)} %param.11) | copy-start | bytes 8257540
  6.5 85.7 %all-gather.5.cloned.1.call-start = ((), (), s32[]{:S(2)}) async-start(), calls=%async_computation | async-start | bytes 3244032 | tf_op jit(solution)/shard_map/all_gather | solution.py:84
  7.3 124.2 %all-gather.9.cloned.1.call-start = ((), (), s32[]{:S(2)}) async-start(), calls=%async_computation.2 | async-start | bytes 4718592 | tf_op jit(solution)/shard_map/all_gather | solution.py:12
  96.3 5.1 %copy-start.3 = (f32[128]{0:T(128)S(1)}, f32[128]{0:T(128)}, u32[]{:S(2)}) copy-start(f32[128]{0:T(128)} %param.15) | copy-start | bytes 1540
  96.4 110.3 %all-gather.7.cloned.1.call-start = ((), (), s32[]{:S(2)}) async-start(), calls=%async_computation.1 | async-start | bytes 1081344 | tf_op jit(solution)/shard_map/all_gather | solution.py:85
  101.4 22.2 %copy-start.5 = (s32[16]{0:T(128)S(1)}, s32[16]{0:T(128)}, u32[]{:S(2)}) copy-start(s32[16]{0:T(128)} %param.19) | copy-start | bytes 196
  102.1 0.6 copy-start.1
  102.1 1.3 copy-start.2
  103.3 112.0 %collective-permute-start.2 = (bf16[512,1,128]{0,2,1:T(8,128)(2,1)}, bf16[512,1,128]{0,2,1:T(8,128)(2,1)}, u32[]{:S(2)}, u32[]{:S(2)}) collective-permute-start(bf16[512,1,128]{0,2,1:T(8,128)(2,1)} %pad_maximum_fusion), channel_id=1, source_target_pairs={{0,16},{8,24},{16,32},{24,40},{32,48},{40,56},{48,64},{56,72},{64,... | collective-permute-start | bytes 393224 | tf_op jit(solution)/shard_map/ppermute | solution.py:21
  107.2 108.1 %collective-permute-start.3 = (bf16[512,1,128]{0,2,1:T(8,128)(2,1)}, bf16[512,1,128]{0,2,1:T(8,128)(2,1)}, u32[]{:S(2)}, u32[]{:S(2)}) collective-permute-start(bf16[512,1,128]{0,2,1:T(8,128)(2,1)} %pad_maximum_fusion), channel_id=1, source_target_pairs={{0,8},{8,16},{16,24},{24,32},{32,40},{40,48},{48,56},{56,64},{64,7... | collective-permute-start | bytes 393224 | tf_op jit(solution)/shard_map/ppermute | solution.py:21
  117.2 102.3 %collective-permute-start = (bf16[512,128]{1,0:T(8,128)(2,1)}, bf16[512,128]{1,0:T(8,128)(2,1)}, u32[]{:S(2)}, u32[]{:S(2)}) collective-permute-start(bf16[512,128]{1,0:T(8,128)(2,1)} %convolution_convert_fusion.1), channel_id=1, source_target_pairs={{0,16},{8,24},{16,32},{24,40},{32,48},{40,56},{48,64},{56,72},{64,... | collective-permute-start | bytes 393224 | tf_op jit(solution)/shard_map/ppermute | solution.py:21
  119.9 99.6 %collective-permute-start.1 = (bf16[512,128]{1,0:T(8,128)(2,1)}, bf16[512,128]{1,0:T(8,128)(2,1)}, u32[]{:S(2)}, u32[]{:S(2)}) collective-permute-start(bf16[512,128]{1,0:T(8,128)(2,1)} %convolution_convert_fusion.1), channel_id=1, source_target_pairs={{0,8},{8,16},{16,24},{24,32},{32,40},{40,48},{48,56},{56,64},{64,7... | collective-permute-start | bytes 393224 | tf_op jit(solution)/shard_map/ppermute | solution.py:21
  131.5 81.3 %copy-start.4 = (f32[128]{0:T(128)S(1)}, f32[128]{0:T(128)}, u32[]{:S(2)}) copy-start(f32[128]{0:T(128)} %param.14) | copy-start | bytes 1540
Sparse Core Ops, SparseCore 0:
  9.9 82.2 all-gather.4
  96.5 30.2 all-gather.8
  129.3 77.2 all-gather.6
